TPU v7x, 256 devices: a whole 4x4x8 slice. The times are simulated.
256 devices in a mesh: section: 8 (over z), lon: 32 (over y, x, core).
Axes of the slice: x: 4, y: 4, z: 8, core: 2. Of those that a mesh axis runs over, the one named last changes fastest.
Arguments:
- lanczos_block: bfloat16 [16, 8, 256, 512], P(None, None, 'lon'), may hold values from -9 to 9
- previous: bfloat16 [16, 8, 256, 512], P(None, 'section', 'lon'), may hold values from -6 to 6
- beta_prev: float32 [16, 16], replicated, may hold values from -2 to 2, as said below
- weights: bfloat16 [8, 9, 512, 512], P('section'), may hold values from -0.09375 to 0.09375
- act_slope: bfloat16 [8, 8, 256, 512], P('section', None, 'lon'), may hold values from 0 to 1.09375
- metric: float32 [8, 256], P(None, 'lon'), may hold values from 0.3 to 3
Outputs:
- residual_block: float32 [16, 8, 256, 512], P(None, 'section', 'lon')
- projection: float32 [16, 16], replicated
- residual_gram: float32 [16, 16], replicated
Inputs may be any that keep to these rules, and one draw needn't show every extreme that they name: `beta_prev`: upper triangular, with a positive diagonal.
All inputs are finite; a program needn't handle non-finite values.
Results may differ from a plain program's by a relative error of at most 0.02.
Values may be sent and summed in bfloat16 or wider, within the bound.
No kernel may reach another device: no remote copies, remote signals or barrier semaphores. Data moves between devices by JAX's collectives and lax.ppermute only.
A program may use at most 64 MiB of HBM per device.

v0:
```python
import jax
import jax.numpy as jnp
from jax import lax
from jax.sharding import PartitionSpec as P

K = 16
DILATION_SIZE = 4


def padded(cells, sides, width):
    for axis, dim in sides:
        count = lax.axis_size(axis)
        head = lax.slice_in_dim(cells, 0, width, axis=dim)
        tail = lax.slice_in_dim(cells, cells.shape[dim] - width, cells.shape[dim], axis=dim)
        cells = jnp.concatenate(
            [
                lax.ppermute(tail, axis, [(i, (i + 1) % count) for i in range(count)]),
                cells,
                lax.ppermute(head, axis, [((i + 1) % count, i) for i in range(count)]),
            ],
            axis=dim,
        )
    return cells


def from_behind(shard, axis, by):
    count = lax.axis_size(axis)
    pairs = [(i, i + by) for i in range(count) if 0 <= i + by < count]
    return lax.ppermute(shard, axis, pairs)


def broadcast(shard, axis, root):
    mine = lax.axis_index(axis) == root
    return lax.psum(jnp.where(mine, shard, jnp.zeros_like(shard)), axis)


def spread_taps(input_field, tap_weights, direction_sign, border_width):
    micro_size = input_field.shape[0]
    lat_rows = input_field.shape[1]
    lon_cols = input_field.shape[2] - 2 * border_width
    channels = input_field.shape[3]
    padded_field = jnp.pad(input_field, ((0, 0), (border_width, border_width), (0, 0), (0, 0)))
    summed = jnp.zeros((micro_size * lat_rows * lon_cols, channels), jnp.float32)
    for row_stride in (-1, 0, 1):
        for column_stride in (-1, 0, 1):
            tap_index = 3 * (row_stride + 1) + (column_stride + 1)
            first_row = border_width + direction_sign * row_stride * border_width
            col_start = border_width + direction_sign * column_stride * border_width
            tap_rows = padded_field[
                :, first_row : first_row + lat_rows, col_start : col_start + lon_cols, :
            ].reshape(-1, channels)
            if direction_sign > 0:
                summed = summed + jnp.dot(
                    tap_rows, tap_weights[tap_index], preferred_element_type=jnp.float32
                )
            else:
                summed = summed + lax.dot_general(
                    tap_rows,
                    tap_weights[tap_index],
                    (((1,), (1,)), ((), ())),
                    preferred_element_type=jnp.float32,
                )
    return summed.reshape(micro_size, lat_rows, lon_cols, channels)


def body(lanczos_block, previous, beta_prev, weights, act_slope, metric):
    section_count = lax.axis_size("section")
    section_index = lax.axis_index("section")
    tap_weights = weights[0]
    slope_here = act_slope[0].astype(jnp.float32)[None]
    border_width = DILATION_SIZE
    micro_count = 2
    micro_size = K // micro_count
    slot_shape = (micro_size,) + lanczos_block.shape[1:]
    lon_cols = lanczos_block.shape[2]
    micro_feeds = lanczos_block.reshape((micro_count,) + slot_shape)
    tick_count = micro_count + section_count - 1
    zero_slot = jnp.zeros(slot_shape, jnp.bfloat16)
    empty_store = jnp.zeros((micro_count,) + slot_shape, jnp.bfloat16)

    def forward_layer(rimmed):
        convolved = spread_taps(rimmed, tap_weights, 1, border_width)
        centre = rimmed[:, :, border_width : border_width + lon_cols, :].astype(jnp.float32)
        return (centre + slope_here * convolved).astype(jnp.bfloat16)

    def skip_forward(rimmed):
        return zero_slot

    def forward_tick(state_pair, tick_now):
        inbound, forward_out = state_pair
        micro_index = tick_now - section_index
        active = (micro_index >= 0) & (micro_index < micro_count)
        slot_index = jnp.clip(micro_index, 0, micro_count - 1)
        fed_slot = lax.dynamic_index_in_dim(micro_feeds, slot_index, 0, keepdims=False)
        incoming = jnp.where(section_index == 0, fed_slot, inbound)
        rimmed = padded(incoming, (("lon", 2),), border_width)
        result = lax.cond(active, forward_layer, skip_forward, rimmed)
        keep_slot = active & (section_index == section_count - 1)
        old_slot = lax.dynamic_index_in_dim(forward_out, slot_index, 0, keepdims=False)
        forward_out = lax.dynamic_update_index_in_dim(
            forward_out, jnp.where(keep_slot, result, old_slot), slot_index, 0
        )
        outbound = from_behind(result, "section", 1)
        return ((outbound, forward_out), None)

    (unused_slot, forward_out), unused_out = lax.scan(
        forward_tick, (zero_slot, empty_store), jnp.arange(tick_count, dtype=jnp.int32)
    )
    metric_here = metric[None, :, :, None]

    def backward_layer(operands):
        incoming, rimmed = operands
        convolved = spread_taps(rimmed, tap_weights, -1, border_width)
        return (incoming.astype(jnp.float32) + convolved).astype(jnp.bfloat16)

    def skip_backward(operands):
        return zero_slot

    def backward_tick(state_pair, tick_now):
        inbound, adjoint_out = state_pair
        micro_index = tick_now - (section_count - 1 - section_index)
        active = (micro_index >= 0) & (micro_index < micro_count)
        slot_index = jnp.clip(micro_index, 0, micro_count - 1)
        stored_slot = lax.dynamic_index_in_dim(forward_out, slot_index, 0, keepdims=False)
        started = (metric_here * stored_slot.astype(jnp.float32)).astype(jnp.bfloat16)
        incoming = jnp.where(section_index == section_count - 1, started, inbound)
        sensitivity = (slope_here * incoming.astype(jnp.float32)).astype(jnp.bfloat16)
        rimmed = padded(sensitivity, (("lon", 2),), border_width)
        result = lax.cond(active, backward_layer, skip_backward, (incoming, rimmed))
        keep_slot = active & (section_index == 0)
        old_slot = lax.dynamic_index_in_dim(adjoint_out, slot_index, 0, keepdims=False)
        adjoint_out = lax.dynamic_update_index_in_dim(
            adjoint_out, jnp.where(keep_slot, result, old_slot), slot_index, 0
        )
        outbound = from_behind(result, "section", -1)
        return ((outbound, adjoint_out), None)

    (unused_back, adjoint_out), unused_more = lax.scan(
        backward_tick, (zero_slot, empty_store), jnp.arange(tick_count, dtype=jnp.int32)
    )
    applied = adjoint_out.reshape(lanczos_block.shape)
    applied_all = broadcast(applied, "section", 0)
    row_count = previous.shape[1]
    applied_rows = lax.dynamic_slice_in_dim(applied_all, section_index * row_count, row_count, 1)
    own_block = lax.dynamic_slice_in_dim(lanczos_block, section_index * row_count, row_count, 1)
    high = lax.Precision.HIGHEST
    cell_count = (
        lanczos_block.shape[1]
        * lanczos_block.shape[2]
        * lax.axis_size("lon")
        * lanczos_block.shape[3]
    )
    block_flat = own_block.reshape(K, -1).astype(jnp.float32)
    prev_flat = previous.reshape(K, -1).astype(jnp.float32)
    shifted = applied_rows.reshape(K, -1).astype(jnp.float32) - jnp.dot(
        beta_prev, prev_flat, precision=high
    )
    part_projection = jnp.dot(block_flat, shifted.T, precision=high) / cell_count
    projection = lax.psum(part_projection, ("section", "lon"))
    residual_rows = shifted - jnp.dot(projection.T, block_flat, precision=high)
    part_gram = jnp.dot(residual_rows, residual_rows.T, precision=high) / cell_count
    residual_gram = lax.psum(part_gram, ("section", "lon"))
    return (residual_rows.reshape(own_block.shape), projection, residual_gram)


def solution(mesh):
    return jax.shard_map(
        body,
        mesh=mesh,
        in_specs=(
            P(None, None, "lon", None),
            P(None, "section", "lon", None),
            P(),
            P("section", None, None, None),
            P("section", None, "lon", None),
            P(None, "lon"),
        ),
        out_specs=(P(None, "section", "lon", None), P(), P()),
        check_vma=False,
    )
```

profile of v0, /device:TPU:1, one launch (start us, length us, event | category | flops | bytes accessed | tf_op | source)
XLA Modules:
  0.0 797.1 jit_solution(21797135074578725)
XLA Ops:
  8.3 248.3 %while.27 = (s32[]{:T(128)}, bf16[8,8,8,512]{3,2,1,0:T(8,128)(2,1)S(1)}, bf16[2,8,8,8,512]{4,3,2,1,0:T(8,128)(2,1)S(1)}, s32[9]{0:T(128)S(1)}, s32[]{:T(128)}, /...) while((s32[]{:T(128)}, ...), condition=%wide.region_3.4_spmd, body=%wide.region_0.3_spmd.sunk | while | flops 2422734848 | bytes 67240344 | solution.py:106
  18.7 6.5 conditional.4
  26.8 5.8 collective-permute-done.2
  35.1 8.7 %collective-permute-start = (bf16[8,8,4,512]{3,2,1,0:T(4,128)(2,1)S(1)}, bf16[8,8,4,512]{3,2,1,0:T(4,128)(2,1)S(1)}, u32[]{:S(2)}, u32[]{:S(2)}) collective-permute-start(bf16[8,8,4,512]{3,2,1,0:T(4,128)(2,1)S(1)} %get-tuple-element.424), channel_id=1, source_target_pairs={{1,0},{2,1},{3,2},{4,3},{5,4},{6,5},{7,6},{8,7},{9,8},{10,9},{11,1... | collective-permute-start | bytes 786440 | tf_op jit(solution)/shard_map/while/body/eval_jaxpr/ppermute | solution.py:19
  48.4 6.5 conditional.4
  59.0 5.8 collective-permute-done.2
  67.3 9.0 %collective-permute-start = (bf16[8,8,4,512]{3,2,1,0:T(4,128)(2,1)S(1)}, bf16[8,8,4,512]{3,2,1,0:T(4,128)(2,1)S(1)}, u32[]{:S(2)}, u32[]{:S(2)}) collective-permute-start(bf16[8,8,4,512]{3,2,1,0:T(4,128)(2,1)S(1)} %get-tuple-element.424), channel_id=1, source_target_pairs={{1,0},{2,1},{3,2},{4,3},{5,4},{6,5},{7,6},{8,7},{9,8},{10,9},{11,1... | collective-permute-start | bytes 786440 | tf_op jit(solution)/shard_map/while/body/eval_jaxpr/ppermute | solution.py:19
  80.4 10.6 %collective-permute-start.2 = (bf16[8,8,8,512]{3,2,1,0:T(8,128)(2,1)S(1)}, bf16[8,8,8,512]{3,2,1,0:T(8,128)(2,1)S(1)}, u32[]{:S(2)}, u32[]{:S(2)}) collective-permute-start(bf16[8,8,8,512]{3,2,1,0:T(8,128)(2,1)S(1)} %get-tuple-element.522), channel_id=1, source_target_pairs={{0,32},{32,64},{64,96},{96,128},{128,160},{160,192},{192,224},{1,3... | collective-permute-start | bytes 1572872 | tf_op jit(solution)/shard_map/while/body/eval_jaxpr/ppermute | solution.py:29
  91.2 5.8 collective-permute-done.2
  99.6 8.1 %collective-permute-start = (bf16[8,8,4,512]{3,2,1,0:T(4,128)(2,1)S(1)}, bf16[8,8,4,512]{3,2,1,0:T(4,128)(2,1)S(1)}, u32[]{:S(2)}, u32[]{:S(2)}) collective-permute-start(bf16[8,8,4,512]{3,2,1,0:T(4,128)(2,1)S(1)} %get-tuple-element.424), channel_id=1, source_target_pairs={{1,0},{2,1},{3,2},{4,3},{5,4},{6,5},{7,6},{8,7},{9,8},{10,9},{11,1... | collective-permute-start | bytes 786440 | tf_op jit(solution)/shard_map/while/body/eval_jaxpr/ppermute | solution.py:19
  116.1 5.8 collective-permute-done.2
  124.4 7.2 collective-permute-start
  135.7 8.7 %collective-permute-start.2 = (bf16[8,8,8,512]{3,2,1,0:T(8,128)(2,1)S(1)}, bf16[8,8,8,512]{3,2,1,0:T(8,128)(2,1)S(1)}, u32[]{:S(2)}, u32[]{:S(2)}) collective-permute-start(bf16[8,8,8,512]{3,2,1,0:T(8,128)(2,1)S(1)} %get-tuple-element.522), channel_id=1, source_target_pairs={{0,32},{32,64},{64,96},{96,128},{128,160},{160,192},{192,224},{1,3... | collective-permute-start | bytes 1572872 | tf_op jit(solution)/shard_map/while/body/eval_jaxpr/ppermute | solution.py:29
  144.6 5.8 collective-permute-done.2
  152.9 7.4 collective-permute-start
  168.8 5.8 collective-permute-done.2
  177.1 6.8 collective-permute-start
  188.0 8.7 %collective-permute-start.2 = (bf16[8,8,8,512]{3,2,1,0:T(8,128)(2,1)S(1)}, bf16[8,8,8,512]{3,2,1,0:T(8,128)(2,1)S(1)}, u32[]{:S(2)}, u32[]{:S(2)}) collective-permute-start(bf16[8,8,8,512]{3,2,1,0:T(8,128)(2,1)S(1)} %get-tuple-element.522), channel_id=1, source_target_pairs={{0,32},{32,64},{64,96},{96,128},{128,160},{160,192},{192,224},{1,3... | collective-permute-start | bytes 1572872 | tf_op jit(solution)/shard_map/while/body/eval_jaxpr/ppermute | solution.py:29
  196.9 5.8 collective-permute-done.2
  205.2 6.8 collective-permute-start
  220.5 5.8 collective-permute-done.2
  228.8 6.8 collective-permute-start
  239.7 10.7 %collective-permute-start.2 = (bf16[8,8,8,512]{3,2,1,0:T(8,128)(2,1)S(1)}, bf16[8,8,8,512]{3,2,1,0:T(8,128)(2,1)S(1)}, u32[]{:S(2)}, u32[]{:S(2)}) collective-permute-start(bf16[8,8,8,512]{3,2,1,0:T(8,128)(2,1)S(1)} %get-tuple-element.522), channel_id=1, source_target_pairs={{0,32},{32,64},{64,96},{96,128},{128,160},{160,192},{192,224},{1,3... | collective-permute-start | bytes 1572872 | tf_op jit(solution)/shard_map/while/body/eval_jaxpr/ppermute | solution.py:29
  250.7 5.8 collective-permute-done.2
  257.5 306.7 %while.28 = (s32[]{:T(128)}, bf16[8,8,8,512]{3,2,1,0:T(8,128)(2,1)}, bf16[2,8,8,8,512]{4,3,2,1,0:T(8,128)(2,1)S(1)}, s32[9]{0:T(128)S(1)}, s32[]{:T(128)}, /*ind...) while((s32[]{:T(128)}, ...), condition=%wide.region_7.8_spmd, body=%wide.region_4.7_spmd.sunk | while | flops 2424045568 | bytes 67764888 | solution.py:138
  261.0 6.7 collective-permute-start.3
  274.4 10.3 %collective-permute-done.5 = bf16[8,8,8,512]{3,2,1,0:T(8,128)(2,1)} collective-permute-done((bf16[8,8,8,512]{3,2,1,0:T(8,128)(2,1)S(1)}, bf16[8,8,8,512]{3,2,1,0:T(8,128)(2,1)}, u32[]{:S(2)}, u32[]{:S(2)}) %collective-permute-start.5) | collective-permute-done | bytes 524320 | tf_op jit(solution)/shard_map/while/body/eval_jaxpr/ppermute | solution.py:29
  288.2 6.8 collective-permute-start.3
  301.6 12.0 %collective-permute-done.5 = bf16[8,8,8,512]{3,2,1,0:T(8,128)(2,1)} collective-permute-done((bf16[8,8,8,512]{3,2,1,0:T(8,128)(2,1)S(1)}, bf16[8,8,8,512]{3,2,1,0:T(8,128)(2,1)}, u32[]{:S(2)}, u32[]{:S(2)}) %collective-permute-start.5) | collective-permute-done | bytes 524320 | tf_op jit(solution)/shard_map/while/body/eval_jaxpr/ppermute | solution.py:29
  317.2 6.8 collective-permute-start.3
  330.6 10.5 %collective-permute-done.5 = bf16[8,8,8,512]{3,2,1,0:T(8,128)(2,1)} collective-permute-done((bf16[8,8,8,512]{3,2,1,0:T(8,128)(2,1)S(1)}, bf16[8,8,8,512]{3,2,1,0:T(8,128)(2,1)}, u32[]{:S(2)}, u32[]{:S(2)}) %collective-permute-start.5) | collective-permute-done | bytes 524320 | tf_op jit(solution)/shard_map/while/body/eval_jaxpr/ppermute | solution.py:29
  344.6 6.8 collective-permute-start.3
  358.0 12.0 %collective-permute-done.5 = bf16[8,8,8,512]{3,2,1,0:T(8,128)(2,1)} collective-permute-done((bf16[8,8,8,512]{3,2,1,0:T(8,128)(2,1)S(1)}, bf16[8,8,8,512]{3,2,1,0:T(8,128)(2,1)}, u32[]{:S(2)}, u32[]{:S(2)}) %collective-permute-start.5) | collective-permute-done | bytes 524320 | tf_op jit(solution)/shard_map/while/body/eval_jaxpr/ppermute | solution.py:29
  373.6 6.8 collective-permute-start.3
  386.9 10.0 %collective-permute-done.5 = bf16[8,8,8,512]{3,2,1,0:T(8,128)(2,1)} collective-permute-done((bf16[8,8,8,512]{3,2,1,0:T(8,128)(2,1)S(1)}, bf16[8,8,8,512]{3,2,1,0:T(8,128)(2,1)}, u32[]{:S(2)}, u32[]{:S(2)}) %collective-permute-start.5) | collective-permute-done | bytes 524320 | tf_op jit(solution)/shard_map/while/body/eval_jaxpr/ppermute | solution.py:29
  400.5 6.8 collective-permute-start.3
  413.9 12.5 %collective-permute-done.5 = bf16[8,8,8,512]{3,2,1,0:T(8,128)(2,1)} collective-permute-done((bf16[8,8,8,512]{3,2,1,0:T(8,128)(2,1)S(1)}, bf16[8,8,8,512]{3,2,1,0:T(8,128)(2,1)}, u32[]{:S(2)}, u32[]{:S(2)}) %collective-permute-start.5) | collective-permute-done | bytes 524320 | tf_op jit(solution)/shard_map/while/body/eval_jaxpr/ppermute | solution.py:29
  429.9 6.8 collective-permute-start.3
  443.3 54.9 %collective-permute-done.5 = bf16[8,8,8,512]{3,2,1,0:T(8,128)(2,1)} collective-permute-done((bf16[8,8,8,512]{3,2,1,0:T(8,128)(2,1)S(1)}, bf16[8,8,8,512]{3,2,1,0:T(8,128)(2,1)}, u32[]{:S(2)}, u32[]{:S(2)}) %collective-permute-start.5) | collective-permute-done | bytes 524320 | tf_op jit(solution)/shard_map/while/body/eval_jaxpr/ppermute | solution.py:29
  501.8 6.8 collective-permute-start.3
  513.6 6.8 conditional.5
  522.0 10.0 %collective-permute-done.5 = bf16[8,8,8,512]{3,2,1,0:T(8,128)(2,1)} collective-permute-done((bf16[8,8,8,512]{3,2,1,0:T(8,128)(2,1)S(1)}, bf16[8,8,8,512]{3,2,1,0:T(8,128)(2,1)}, u32[]{:S(2)}, u32[]{:S(2)}) %collective-permute-start.5) | collective-permute-done | bytes 524320 | tf_op jit(solution)/shard_map/while/body/eval_jaxpr/ppermute | solution.py:29
  535.5 6.8 collective-permute-start.3
  547.3 6.8 conditional.5
  555.7 8.5 %collective-permute-done.5 = bf16[8,8,8,512]{3,2,1,0:T(8,128)(2,1)} collective-permute-done((bf16[8,8,8,512]{3,2,1,0:T(8,128)(2,1)S(1)}, bf16[8,8,8,512]{3,2,1,0:T(8,128)(2,1)}, u32[]{:S(2)}, u32[]{:S(2)}) %collective-permute-start.5) | collective-permute-done | bytes 524320 | tf_op jit(solution)/shard_map/while/body/eval_jaxpr/ppermute | solution.py:29
  566.4 67.9 %all-reduce.4.cloned.1.call-done = bf16[16,8,8,512]{3,2,0,1:T(8,128)(2,1)} async-done(((bf16[16,8,8,512]{3,2,0,1:T(8,128)(2,1)}), bf16[16,8,8,512]{3,2,0,1:T(8,128)(2,1)}) %all-reduce.4.cloned.1.call-update) | async-done | bytes 1048592 | tf_op jit(solution)/shard_map/psum | solution.py:34
  636.0 79.2 %psum.22 = f32[16,16]{1,0:T(8,128)S(1)} all-reduce(f32[16,16]{1,0:T(8,128)S(1)} %convolution_multiply_fusion.1), channel_id=1, replica_groups=mesh['section'=8,'lon'=32] {'section','lon'}, use_global_device_ids=true, to_apply=%region_9.10 | all-reduce | flops 256 | bytes 2048 | tf_op jit(solution)/shard_map/psum | solution.py:159
  716.9 73.3 %psum.23 = f32[16,16]{1,0:T(8,128)} all-reduce(f32[16,16]{1,0:T(8,128)S(1)} %convolution_multiply_fusion), channel_id=1, replica_groups=mesh['section'=8,'lon'=32] {'section','lon'}, use_global_device_ids=true, to_apply=%region_10.11 | all-reduce | flops 256 | bytes 2048 | tf_op jit(solution)/shard_map/psum | solution.py:162
  (286 shorter events, 196.7 us)
Async XLA Ops:
  7.2 627.2 %all-reduce.4.cloned.1.call-start = ((), (), s32[]{:S(2)}) async-start(), calls=%async_computation | async-start | bytes 2097152 | tf_op jit(solution)/shard_map/psum | solution.py:34
  10.8 6.7 collective-permute-start
  14.0 4.0 collective-permute-start.1
  25.2 7.4 collective-permute-start.2
  35.1 11.0 %collective-permute-start = (bf16[8,8,4,512]{3,2,1,0:T(4,128)(2,1)S(1)}, bf16[8,8,4,512]{3,2,1,0:T(4,128)(2,1)S(1)}, u32[]{:S(2)}, u32[]{:S(2)}) collective-permute-start(bf16[8,8,4,512]{3,2,1,0:T(4,128)(2,1)S(1)} %get-tuple-element.424), channel_id=1, source_target_pairs={{1,0},{2,1},{3,2},{4,3},{5,4},{6,5},{7,6},{8,7},{9,8},{10,9},{11,1... | collective-permute-start | bytes 786440 | tf_op jit(solution)/shard_map/while/body/eval_jaxpr/ppermute | solution.py:19
  43.8 3.9 collective-permute-start.1
  54.9 9.9 %collective-permute-start.2 = (bf16[8,8,8,512]{3,2,1,0:T(8,128)(2,1)S(1)}, bf16[8,8,8,512]{3,2,1,0:T(8,128)(2,1)S(1)}, u32[]{:S(2)}, u32[]{:S(2)}) collective-permute-start(bf16[8,8,8,512]{3,2,1,0:T(8,128)(2,1)S(1)} %get-tuple-element.522), channel_id=1, source_target_pairs={{0,32},{32,64},{64,96},{96,128},{128,160},{160,192},{192,224},{1,3... | collective-permute-start | bytes 1572872 | tf_op jit(solution)/shard_map/while/body/eval_jaxpr/ppermute | solution.py:29
  67.3 10.2 %collective-permute-start = (bf16[8,8,4,512]{3,2,1,0:T(4,128)(2,1)S(1)}, bf16[8,8,4,512]{3,2,1,0:T(4,128)(2,1)S(1)}, u32[]{:S(2)}, u32[]{:S(2)}) collective-permute-start(bf16[8,8,4,512]{3,2,1,0:T(4,128)(2,1)S(1)} %get-tuple-element.424), channel_id=1, source_target_pairs={{1,0},{2,1},{3,2},{4,3},{5,4},{6,5},{7,6},{8,7},{9,8},{10,9},{11,1... | collective-permute-start | bytes 786440 | tf_op jit(solution)/shard_map/while/body/eval_jaxpr/ppermute | solution.py:19
  76.3 3.3 collective-permute-start.1
  80.4 16.7 %collective-permute-start.2 = (bf16[8,8,8,512]{3,2,1,0:T(8,128)(2,1)S(1)}, bf16[8,8,8,512]{3,2,1,0:T(8,128)(2,1)S(1)}, u32[]{:S(2)}, u32[]{:S(2)}) collective-permute-start(bf16[8,8,8,512]{3,2,1,0:T(8,128)(2,1)S(1)} %get-tuple-element.522), channel_id=1, source_target_pairs={{0,32},{32,64},{64,96},{96,128},{128,160},{160,192},{192,224},{1,3... | collective-permute-start | bytes 1572872 | tf_op jit(solution)/shard_map/while/body/eval_jaxpr/ppermute | solution.py:29
  99.6 9.3 %collective-permute-start = (bf16[8,8,4,512]{3,2,1,0:T(4,128)(2,1)S(1)}, bf16[8,8,4,512]{3,2,1,0:T(4,128)(2,1)S(1)}, u32[]{:S(2)}, u32[]{:S(2)}) collective-permute-start(bf16[8,8,4,512]{3,2,1,0:T(4,128)(2,1)S(1)} %get-tuple-element.424), channel_id=1, source_target_pairs={{1,0},{2,1},{3,2},{4,3},{5,4},{6,5},{7,6},{8,7},{9,8},{10,9},{11,1... | collective-permute-start | bytes 786440 | tf_op jit(solution)/shard_map/while/body/eval_jaxpr/ppermute | solution.py:19
  107.7 3.3 collective-permute-start.1
  111.7 10.2 %collective-permute-start.2 = (bf16[8,8,8,512]{3,2,1,0:T(8,128)(2,1)S(1)}, bf16[8,8,8,512]{3,2,1,0:T(8,128)(2,1)S(1)}, u32[]{:S(2)}, u32[]{:S(2)}) collective-permute-start(bf16[8,8,8,512]{3,2,1,0:T(8,128)(2,1)S(1)} %get-tuple-element.522), channel_id=1, source_target_pairs={{0,32},{32,64},{64,96},{96,128},{128,160},{160,192},{192,224},{1,3... | collective-permute-start | bytes 1572872 | tf_op jit(solution)/shard_map/while/body/eval_jaxpr/ppermute | solution.py:29
  124.4 8.3 %collective-permute-start = (bf16[8,8,4,512]{3,2,1,0:T(4,128)(2,1)S(1)}, bf16[8,8,4,512]{3,2,1,0:T(4,128)(2,1)S(1)}, u32[]{:S(2)}, u32[]{:S(2)}) collective-permute-start(bf16[8,8,4,512]{3,2,1,0:T(4,128)(2,1)S(1)} %get-tuple-element.424), channel_id=1, source_target_pairs={{1,0},{2,1},{3,2},{4,3},{5,4},{6,5},{7,6},{8,7},{9,8},{10,9},{11,1... | collective-permute-start | bytes 786440 | tf_op jit(solution)/shard_map/while/body/eval_jaxpr/ppermute | solution.py:19
  131.6 3.3 collective-permute-start.1
  135.7 14.8 %collective-permute-start.2 = (bf16[8,8,8,512]{3,2,1,0:T(8,128)(2,1)S(1)}, bf16[8,8,8,512]{3,2,1,0:T(8,128)(2,1)S(1)}, u32[]{:S(2)}, u32[]{:S(2)}) collective-permute-start(bf16[8,8,8,512]{3,2,1,0:T(8,128)(2,1)S(1)} %get-tuple-element.522), channel_id=1, source_target_pairs={{0,32},{32,64},{64,96},{96,128},{128,160},{160,192},{192,224},{1,3... | collective-permute-start | bytes 1572872 | tf_op jit(solution)/shard_map/while/body/eval_jaxpr/ppermute | solution.py:29
  152.9 8.6 %collective-permute-start = (bf16[8,8,4,512]{3,2,1,0:T(4,128)(2,1)S(1)}, bf16[8,8,4,512]{3,2,1,0:T(4,128)(2,1)S(1)}, u32[]{:S(2)}, u32[]{:S(2)}) collective-permute-start(bf16[8,8,4,512]{3,2,1,0:T(4,128)(2,1)S(1)} %get-tuple-element.424), channel_id=1, source_target_pairs={{1,0},{2,1},{3,2},{4,3},{5,4},{6,5},{7,6},{8,7},{9,8},{10,9},{11,1... | collective-permute-start | bytes 786440 | tf_op jit(solution)/shard_map/while/body/eval_jaxpr/ppermute | solution.py:19
  160.3 3.3 collective-permute-start.1
  164.4 10.2 %collective-permute-start.2 = (bf16[8,8,8,512]{3,2,1,0:T(8,128)(2,1)S(1)}, bf16[8,8,8,512]{3,2,1,0:T(8,128)(2,1)S(1)}, u32[]{:S(2)}, u32[]{:S(2)}) collective-permute-start(bf16[8,8,8,512]{3,2,1,0:T(8,128)(2,1)S(1)} %get-tuple-element.522), channel_id=1, source_target_pairs={{0,32},{32,64},{64,96},{96,128},{128,160},{160,192},{192,224},{1,3... | collective-permute-start | bytes 1572872 | tf_op jit(solution)/shard_map/while/body/eval_jaxpr/ppermute | solution.py:29
  177.1 8.0 %collective-permute-start = (bf16[8,8,4,512]{3,2,1,0:T(4,128)(2,1)S(1)}, bf16[8,8,4,512]{3,2,1,0:T(4,128)(2,1)S(1)}, u32[]{:S(2)}, u32[]{:S(2)}) collective-permute-start(bf16[8,8,4,512]{3,2,1,0:T(4,128)(2,1)S(1)} %get-tuple-element.424), channel_id=1, source_target_pairs={{1,0},{2,1},{3,2},{4,3},{5,4},{6,5},{7,6},{8,7},{9,8},{10,9},{11,1... | collective-permute-start | bytes 786440 | tf_op jit(solution)/shard_map/while/body/eval_jaxpr/ppermute | solution.py:19
  183.9 3.3 collective-permute-start.1
  188.0 14.8 %collective-permute-start.2 = (bf16[8,8,8,512]{3,2,1,0:T(8,128)(2,1)S(1)}, bf16[8,8,8,512]{3,2,1,0:T(8,128)(2,1)S(1)}, u32[]{:S(2)}, u32[]{:S(2)}) collective-permute-start(bf16[8,8,8,512]{3,2,1,0:T(8,128)(2,1)S(1)} %get-tuple-element.522), channel_id=1, source_target_pairs={{0,32},{32,64},{64,96},{96,128},{128,160},{160,192},{192,224},{1,3... | collective-permute-start | bytes 1572872 | tf_op jit(solution)/shard_map/while/body/eval_jaxpr/ppermute | solution.py:29
  205.2 8.0 %collective-permute-start = (bf16[8,8,4,512]{3,2,1,0:T(4,128)(2,1)S(1)}, bf16[8,8,4,512]{3,2,1,0:T(4,128)(2,1)S(1)}, u32[]{:S(2)}, u32[]{:S(2)}) collective-permute-start(bf16[8,8,4,512]{3,2,1,0:T(4,128)(2,1)S(1)} %get-tuple-element.424), channel_id=1, source_target_pairs={{1,0},{2,1},{3,2},{4,3},{5,4},{6,5},{7,6},{8,7},{9,8},{10,9},{11,1... | collective-permute-start | bytes 786440 | tf_op jit(solution)/shard_map/while/body/eval_jaxpr/ppermute | solution.py:19
  212.0 3.3 collective-permute-start.1
  216.1 10.2 %collective-permute-start.2 = (bf16[8,8,8,512]{3,2,1,0:T(8,128)(2,1)S(1)}, bf16[8,8,8,512]{3,2,1,0:T(8,128)(2,1)S(1)}, u32[]{:S(2)}, u32[]{:S(2)}) collective-permute-start(bf16[8,8,8,512]{3,2,1,0:T(8,128)(2,1)S(1)} %get-tuple-element.522), channel_id=1, source_target_pairs={{0,32},{32,64},{64,96},{96,128},{128,160},{160,192},{192,224},{1,3... | collective-permute-start | bytes 1572872 | tf_op jit(solution)/shard_map/while/body/eval_jaxpr/ppermute | solution.py:29
  228.8 8.0 %collective-permute-start = (bf16[8,8,4,512]{3,2,1,0:T(4,128)(2,1)S(1)}, bf16[8,8,4,512]{3,2,1,0:T(4,128)(2,1)S(1)}, u32[]{:S(2)}, u32[]{:S(2)}) collective-permute-start(bf16[8,8,4,512]{3,2,1,0:T(4,128)(2,1)S(1)} %get-tuple-element.424), channel_id=1, source_target_pairs={{1,0},{2,1},{3,2},{4,3},{5,4},{6,5},{7,6},{8,7},{9,8},{10,9},{11,1... | collective-permute-start | bytes 786440 | tf_op jit(solution)/shard_map/while/body/eval_jaxpr/ppermute | solution.py:19
  235.6 3.3 collective-permute-start.1
  239.7 16.8 %collective-permute-start.2 = (bf16[8,8,8,512]{3,2,1,0:T(8,128)(2,1)S(1)}, bf16[8,8,8,512]{3,2,1,0:T(8,128)(2,1)S(1)}, u32[]{:S(2)}, u32[]{:S(2)}) collective-permute-start(bf16[8,8,8,512]{3,2,1,0:T(8,128)(2,1)S(1)} %get-tuple-element.522), channel_id=1, source_target_pairs={{0,32},{32,64},{64,96},{96,128},{128,160},{160,192},{192,224},{1,3... | collective-permute-start | bytes 1572872 | tf_op jit(solution)/shard_map/while/body/eval_jaxpr/ppermute | solution.py:29
  261.0 8.2 %collective-permute-start.3 = (bf16[8,8,4,512]{3,2,1,0:T(4,128)(2,1)}, bf16[8,8,4,512]{3,2,1,0:T(4,128)(2,1)}, u32[]{:S(2)}, u32[]{:S(2)}) collective-permute-start(bf16[8,8,4,512]{3,2,1,0:T(4,128)(2,1)} %get-tuple-element.439), channel_id=1, source_target_pairs={{1,0},{2,1},{3,2},{4,3},{5,4},{6,5},{7,6},{8,7},{9,8},{10,9},{11,1... | collective-permute-start | bytes 786440 | tf_op jit(solution)/shard_map/while/body/eval_jaxpr/ppermute | solution.py:19
  267.8 3.3 collective-permute-start.4
  272.8 11.8 %collective-permute-start.5 = (bf16[8,8,8,512]{3,2,1,0:T(8,128)(2,1)S(1)}, bf16[8,8,8,512]{3,2,1,0:T(8,128)(2,1)}, u32[]{:S(2)}, u32[]{:S(2)}) collective-permute-start(bf16[8,8,8,512]{3,2,1,0:T(8,128)(2,1)S(1)} %get-tuple-element.523), channel_id=1, source_target_pairs={{32,0},{64,32},{96,64},{128,96},{160,128},{192,160},{224,192},{33,... | collective-permute-start | bytes 1572872 | tf_op jit(solution)/shard_map/while/body/eval_jaxpr/ppermute | solution.py:29
  288.2 8.3 %collective-permute-start.3 = (bf16[8,8,4,512]{3,2,1,0:T(4,128)(2,1)}, bf16[8,8,4,512]{3,2,1,0:T(4,128)(2,1)}, u32[]{:S(2)}, u32[]{:S(2)}) collective-permute-start(bf16[8,8,4,512]{3,2,1,0:T(4,128)(2,1)} %get-tuple-element.439), channel_id=1, source_target_pairs={{1,0},{2,1},{3,2},{4,3},{5,4},{6,5},{7,6},{8,7},{9,8},{10,9},{11,1... | collective-permute-start | bytes 786440 | tf_op jit(solution)/shard_map/while/body/eval_jaxpr/ppermute | solution.py:19
  295.0 3.3 collective-permute-start.4
  300.1 13.6 %collective-permute-start.5 = (bf16[8,8,8,512]{3,2,1,0:T(8,128)(2,1)S(1)}, bf16[8,8,8,512]{3,2,1,0:T(8,128)(2,1)}, u32[]{:S(2)}, u32[]{:S(2)}) collective-permute-start(bf16[8,8,8,512]{3,2,1,0:T(8,128)(2,1)S(1)} %get-tuple-element.523), channel_id=1, source_target_pairs={{32,0},{64,32},{96,64},{128,96},{160,128},{192,160},{224,192},{33,... | collective-permute-start | bytes 1572872 | tf_op jit(solution)/shard_map/while/body/eval_jaxpr/ppermute | solution.py:29
  317.2 8.3 %collective-permute-start.3 = (bf16[8,8,4,512]{3,2,1,0:T(4,128)(2,1)}, bf16[8,8,4,512]{3,2,1,0:T(4,128)(2,1)}, u32[]{:S(2)}, u32[]{:S(2)}) collective-permute-start(bf16[8,8,4,512]{3,2,1,0:T(4,128)(2,1)} %get-tuple-element.439), channel_id=1, source_target_pairs={{1,0},{2,1},{3,2},{4,3},{5,4},{6,5},{7,6},{8,7},{9,8},{10,9},{11,1... | collective-permute-start | bytes 786440 | tf_op jit(solution)/shard_map/while/body/eval_jaxpr/ppermute | solution.py:19
  329.0 12.0 %collective-permute-start.5 = (bf16[8,8,8,512]{3,2,1,0:T(8,128)(2,1)S(1)}, bf16[8,8,8,512]{3,2,1,0:T(8,128)(2,1)}, u32[]{:S(2)}, u32[]{:S(2)}) collective-permute-start(bf16[8,8,8,512]{3,2,1,0:T(8,128)(2,1)S(1)} %get-tuple-element.523), channel_id=1, source_target_pairs={{32,0},{64,32},{96,64},{128,96},{160,128},{192,160},{224,192},{33,... | collective-permute-start | bytes 1572872 | tf_op jit(solution)/shard_map/while/body/eval_jaxpr/ppermute | solution.py:29
  344.6 8.3 %collective-permute-start.3 = (bf16[8,8,4,512]{3,2,1,0:T(4,128)(2,1)}, bf16[8,8,4,512]{3,2,1,0:T(4,128)(2,1)}, u32[]{:S(2)}, u32[]{:S(2)}) collective-permute-start(bf16[8,8,4,512]{3,2,1,0:T(4,128)(2,1)} %get-tuple-element.439), channel_id=1, source_target_pairs={{1,0},{2,1},{3,2},{4,3},{5,4},{6,5},{7,6},{8,7},{9,8},{10,9},{11,1... | collective-permute-start | bytes 786440 | tf_op jit(solution)/shard_map/while/body/eval_jaxpr/ppermute | solution.py:19
  356.4 13.6 %collective-permute-start.5 = (bf16[8,8,8,512]{3,2,1,0:T(8,128)(2,1)S(1)}, bf16[8,8,8,512]{3,2,1,0:T(8,128)(2,1)}, u32[]{:S(2)}, u32[]{:S(2)}) collective-permute-start(bf16[8,8,8,512]{3,2,1,0:T(8,128)(2,1)S(1)} %get-tuple-element.523), channel_id=1, source_target_pairs={{32,0},{64,32},{96,64},{128,96},{160,128},{192,160},{224,192},{33,... | collective-permute-start | bytes 1572872 | tf_op jit(solution)/shard_map/while/body/eval_jaxpr/ppermute | solution.py:29
  373.6 8.3 %collective-permute-start.3 = (bf16[8,8,4,512]{3,2,1,0:T(4,128)(2,1)}, bf16[8,8,4,512]{3,2,1,0:T(4,128)(2,1)}, u32[]{:S(2)}, u32[]{:S(2)}) collective-permute-start(bf16[8,8,4,512]{3,2,1,0:T(4,128)(2,1)} %get-tuple-element.439), channel_id=1, source_target_pairs={{1,0},{2,1},{3,2},{4,3},{5,4},{6,5},{7,6},{8,7},{9,8},{10,9},{11,1... | collective-permute-start | bytes 786440 | tf_op jit(solution)/shard_map/while/body/eval_jaxpr/ppermute | solution.py:19
  385.4 11.5 %collective-permute-start.5 = (bf16[8,8,8,512]{3,2,1,0:T(8,128)(2,1)S(1)}, bf16[8,8,8,512]{3,2,1,0:T(8,128)(2,1)}, u32[]{:S(2)}, u32[]{:S(2)}) collective-permute-start(bf16[8,8,8,512]{3,2,1,0:T(8,128)(2,1)S(1)} %get-tuple-element.523), channel_id=1, source_target_pairs={{32,0},{64,32},{96,64},{128,96},{160,128},{192,160},{224,192},{33,... | collective-permute-start | bytes 1572872 | tf_op jit(solution)/shard_map/while/body/eval_jaxpr/ppermute | solution.py:29
  400.5 8.3 %collective-permute-start.3 = (bf16[8,8,4,512]{3,2,1,0:T(4,128)(2,1)}, bf16[8,8,4,512]{3,2,1,0:T(4,128)(2,1)}, u32[]{:S(2)}, u32[]{:S(2)}) collective-permute-start(bf16[8,8,4,512]{3,2,1,0:T(4,128)(2,1)} %get-tuple-element.439), channel_id=1, source_target_pairs={{1,0},{2,1},{3,2},{4,3},{5,4},{6,5},{7,6},{8,7},{9,8},{10,9},{11,1... | collective-permute-start | bytes 786440 | tf_op jit(solution)/shard_map/while/body/eval_jaxpr/ppermute | solution.py:19
  412.4 14.0 %collective-permute-start.5 = (bf16[8,8,8,512]{3,2,1,0:T(8,128)(2,1)S(1)}, bf16[8,8,8,512]{3,2,1,0:T(8,128)(2,1)}, u32[]{:S(2)}, u32[]{:S(2)}) collective-permute-start(bf16[8,8,8,512]{3,2,1,0:T(8,128)(2,1)S(1)} %get-tuple-element.523), channel_id=1, source_target_pairs={{32,0},{64,32},{96,64},{128,96},{160,128},{192,160},{224,192},{33,... | collective-permute-start | bytes 1572872 | tf_op jit(solution)/shard_map/while/body/eval_jaxpr/ppermute | solution.py:29
  429.9 8.3 %collective-permute-start.3 = (bf16[8,8,4,512]{3,2,1,0:T(4,128)(2,1)}, bf16[8,8,4,512]{3,2,1,0:T(4,128)(2,1)}, u32[]{:S(2)}, u32[]{:S(2)}) collective-permute-start(bf16[8,8,4,512]{3,2,1,0:T(4,128)(2,1)} %get-tuple-element.439), channel_id=1, source_target_pairs={{1,0},{2,1},{3,2},{4,3},{5,4},{6,5},{7,6},{8,7},{9,8},{10,9},{11,1... | collective-permute-start | bytes 786440 | tf_op jit(solution)/shard_map/while/body/eval_jaxpr/ppermute | solution.py:19
  441.8 56.5 %collective-permute-start.5 = (bf16[8,8,8,512]{3,2,1,0:T(8,128)(2,1)S(1)}, bf16[8,8,8,512]{3,2,1,0:T(8,128)(2,1)}, u32[]{:S(2)}, u32[]{:S(2)}) collective-permute-start(bf16[8,8,8,512]{3,2,1,0:T(8,128)(2,1)S(1)} %get-tuple-element.523), channel_id=1, source_target_pairs={{32,0},{64,32},{96,64},{128,96},{160,128},{192,160},{224,192},{33,... | collective-permute-start | bytes 1572872 | tf_op jit(solution)/shard_map/while/body/eval_jaxpr/ppermute | solution.py:29
  501.8 8.3 %collective-permute-start.3 = (bf16[8,8,4,512]{3,2,1,0:T(4,128)(2,1)}, bf16[8,8,4,512]{3,2,1,0:T(4,128)(2,1)}, u32[]{:S(2)}, u32[]{:S(2)}) collective-permute-start(bf16[8,8,4,512]{3,2,1,0:T(4,128)(2,1)} %get-tuple-element.439), channel_id=1, source_target_pairs={{1,0},{2,1},{3,2},{4,3},{5,4},{6,5},{7,6},{8,7},{9,8},{10,9},{11,1... | collective-permute-start | bytes 786440 | tf_op jit(solution)/shard_map/while/body/eval_jaxpr/ppermute | solution.py:19
  520.4 11.5 %collective-permute-start.5 = (bf16[8,8,8,512]{3,2,1,0:T(8,128)(2,1)S(1)}, bf16[8,8,8,512]{3,2,1,0:T(8,128)(2,1)}, u32[]{:S(2)}, u32[]{:S(2)}) collective-permute-start(bf16[8,8,8,512]{3,2,1,0:T(8,128)(2,1)S(1)} %get-tuple-element.523), channel_id=1, source_target_pairs={{32,0},{64,32},{96,64},{128,96},{160,128},{192,160},{224,192},{33,... | collective-permute-start | bytes 1572872 | tf_op jit(solution)/shard_map/while/body/eval_jaxpr/ppermute | solution.py:29
  535.5 8.3 %collective-permute-start.3 = (bf16[8,8,4,512]{3,2,1,0:T(4,128)(2,1)}, bf16[8,8,4,512]{3,2,1,0:T(4,128)(2,1)}, u32[]{:S(2)}, u32[]{:S(2)}) collective-permute-start(bf16[8,8,4,512]{3,2,1,0:T(4,128)(2,1)} %get-tuple-element.439), channel_id=1, source_target_pairs={{1,0},{2,1},{3,2},{4,3},{5,4},{6,5},{7,6},{8,7},{9,8},{10,9},{11,1... | collective-permute-start | bytes 786440 | tf_op jit(solution)/shard_map/while/body/eval_jaxpr/ppermute | solution.py:19
  554.2 10.0 %collective-permute-start.5 = (bf16[8,8,8,512]{3,2,1,0:T(8,128)(2,1)S(1)}, bf16[8,8,8,512]{3,2,1,0:T(8,128)(2,1)}, u32[]{:S(2)}, u32[]{:S(2)}) collective-permute-start(bf16[8,8,8,512]{3,2,1,0:T(8,128)(2,1)S(1)} %get-tuple-element.523), channel_id=1, source_target_pairs={{32,0},{64,32},{96,64},{128,96},{160,128},{192,160},{224,192},{33,... | collective-permute-start | bytes 1572872 | tf_op jit(solution)/shard_map/while/body/eval_jaxpr/ppermute | solution.py:29
  (15 other events, 986.3 us)
Sparse Core Ops, SparseCore 0:
  565.5 68.8 all-reduce.3
where the time goes:
time: 799 us; the launch traced here: 797 us
  waiting for transfers between devices  322 us (40%)
  starting transfers between devices  193 us (24%)
  blocking collectives  153 us (19%)
  other arithmetic  49.3 us (6%)
  local copies, waits for them, and re-layouts  35.4 us (4%)
  matrix products  17.6 us (2%)
  between operations  14.2 us (2%)
  loops' own time  12.5 us (2%)
    ppermute x18, waiting for transfers between devices, from_behind(): return lax.ppermute(shard, axis, pairs)  193 us
    ppermute x18, starting transfers between devices, padded(): lax.ppermute(head, axis, [((i + 1) % count, i) for i in range(count)])  125 us
    psum x1, blocking collectives, body(): projection = lax.psum(part_projection, ('section', 'lon'))  79.2 us
    psum x1, blocking collectives, body(): residual_gram = lax.psum(part_gram, ('section', 'lon'))  73.3 us
    psum x1, waiting for transfers between devices, broadcast(): return lax.psum(jnp.where(mine, shard, jnp.zeros_like(shard)), axis)  67.9 us
    ppermute x18, starting transfers between devices, from_behind(): return lax.ppermute(shard, axis, pairs)  67.9 us
    ppermute x18, waiting for transfers between devices, padded(): lax.ppermute(tail, axis, [(i, (i + 1) % count) for i in range(count)])  33.5 us
    ppermute x18, waiting for transfers between devices, padded(): lax.ppermute(head, axis, [((i + 1) % count, i) for i in range(count)])  27.4 us
  transfers between devices with their start and end apart: 55, of which 55 were waited for; matrix products, arithmetic and copies ran while one was open for 1% of the time, Pallas kernels for 0%

commit v1 on v0

--- a/solution.py
+++ b/solution.py
@@ -159,7 +159,7 @@
     projection = lax.psum(part_projection, ("section", "lon"))
     residual_rows = shifted - jnp.dot(projection.T, block_flat, precision=high)
     part_gram = jnp.dot(residual_rows, residual_rows.T, precision=high) / cell_count
-    residual_gram = lax.psum(part_gram, ("section", "lon"))
+    residual_gram = lax.psum(lax.psum(part_gram, "section"), "lon")
     return (residual_rows.reshape(own_block.shape), projection, residual_gram)
 
 

time: 799 us -> 807 us (1.010)
    psum x1 -> x2, blocking collectives: 73.3 us -> 79.6 us  [body(): residual_gram = lax.psum(lax.psum(part_gram, 'section'), 'lon')]
where the time goes in v1:
time: 807 us; the launch traced here: 805 us
  waiting for transfers between devices  322 us (40%)
  starting transfers between devices  193 us (24%)
  blocking collectives  159 us (20%)
  other arithmetic  49.3 us (6%)
  local copies, waits for them, and re-layouts  36 us (4%)
  matrix products  17.6 us (2%)
  between operations  14.2 us (2%)
  loops' own time  13.3 us (2%)
    ppermute x18, waiting for transfers between devices, from_behind(): return lax.ppermute(shard, axis, pairs)  193 us
    ppermute x18, starting transfers between devices, padded(): lax.ppermute(head, axis, [((i + 1) % count, i) for i in range(count)])  125 us
    psum x2, blocking collectives, body(): residual_gram = lax.psum(lax.psum(part_gram, 'section'), 'lon')  79.6 us
    psum x1, blocking collectives, body(): projection = lax.psum(part_projection, ('section', 'lon'))  79.2 us
    ppermute x18, starting transfers between devices, from_behind(): return lax.ppermute(shard, axis, pairs)  67.9 us
    psum x1, waiting for transfers between devices, broadcast(): return lax.psum(jnp.where(mine, shard, jnp.zeros_like(shard)), axis)  67.9 us
    ppermute x18, waiting for transfers between devices, padded(): lax.ppermute(tail, axis, [(i, (i + 1) % count) for i in range(count)])  33.5 us
    ppermute x18, waiting for transfers between devices, padded(): lax.ppermute(head, axis, [((i + 1) % count, i) for i in range(count)])  27.4 us
  transfers between devices with their start and end apart: 55, of which 55 were waited for; matrix products, arithmetic and copies ran while one was open for 1% of the time, Pallas kernels for 0%

profile of v1, /device:TPU:1, one launch (start us, length us, event | category | flops | bytes accessed | tf_op | source)
XLA Modules:
  0.0 804.6 jit_solution(9021814714355442907)
XLA Ops:
  8.3 249.6 %while.27 = (s32[]{:T(128)}, bf16[8,8,8,512]{3,2,1,0:T(8,128)(2,1)S(1)}, bf16[2,8,8,8,512]{4,3,2,1,0:T(8,128)(2,1)S(1)}, s32[9]{0:T(128)S(1)}, s32[]{:T(128)}, /...) while((s32[]{:T(128)}, ...), condition=%wide.region_3.4_spmd, body=%wide.region_0.3_spmd.sunk | while | flops 2422734848 | bytes 67240344 | solution.py:106
  18.8 6.5 conditional.4
  26.9 5.8 collective-permute-done.2
  35.4 8.7 %collective-permute-start = (bf16[8,8,4,512]{3,2,1,0:T(4,128)(2,1)S(1)}, bf16[8,8,4,512]{3,2,1,0:T(4,128)(2,1)S(1)}, u32[]{:S(2)}, u32[]{:S(2)}) collective-permute-start(bf16[8,8,4,512]{3,2,1,0:T(4,128)(2,1)S(1)} %get-tuple-element.424), channel_id=1, source_target_pairs={{1,0},{2,1},{3,2},{4,3},{5,4},{6,5},{7,6},{8,7},{9,8},{10,9},{11,1... | collective-permute-start | bytes 786440 | tf_op jit(solution)/shard_map/while/body/eval_jaxpr/ppermute | solution.py:19
  48.7 6.5 conditional.4
  59.3 5.8 collective-permute-done.2
  67.8 9.0 %collective-permute-start = (bf16[8,8,4,512]{3,2,1,0:T(4,128)(2,1)S(1)}, bf16[8,8,4,512]{3,2,1,0:T(4,128)(2,1)S(1)}, u32[]{:S(2)}, u32[]{:S(2)}) collective-permute-start(bf16[8,8,4,512]{3,2,1,0:T(4,128)(2,1)S(1)} %get-tuple-element.424), channel_id=1, source_target_pairs={{1,0},{2,1},{3,2},{4,3},{5,4},{6,5},{7,6},{8,7},{9,8},{10,9},{11,1... | collective-permute-start | bytes 786440 | tf_op jit(solution)/shard_map/while/body/eval_jaxpr/ppermute | solution.py:19
  80.9 10.6 %collective-permute-start.2 = (bf16[8,8,8,512]{3,2,1,0:T(8,128)(2,1)S(1)}, bf16[8,8,8,512]{3,2,1,0:T(8,128)(2,1)S(1)}, u32[]{:S(2)}, u32[]{:S(2)}) collective-permute-start(bf16[8,8,8,512]{3,2,1,0:T(8,128)(2,1)S(1)} %get-tuple-element.522), channel_id=1, source_target_pairs={{0,32},{32,64},{64,96},{96,128},{128,160},{160,192},{192,224},{1,3... | collective-permute-start | bytes 1572872 | tf_op jit(solution)/shard_map/while/body/eval_jaxpr/ppermute | solution.py:29
  91.7 5.8 collective-permute-done.2
  100.2 8.1 %collective-permute-start = (bf16[8,8,4,512]{3,2,1,0:T(4,128)(2,1)S(1)}, bf16[8,8,4,512]{3,2,1,0:T(4,128)(2,1)S(1)}, u32[]{:S(2)}, u32[]{:S(2)}) collective-permute-start(bf16[8,8,4,512]{3,2,1,0:T(4,128)(2,1)S(1)} %get-tuple-element.424), channel_id=1, source_target_pairs={{1,0},{2,1},{3,2},{4,3},{5,4},{6,5},{7,6},{8,7},{9,8},{10,9},{11,1... | collective-permute-start | bytes 786440 | tf_op jit(solution)/shard_map/while/body/eval_jaxpr/ppermute | solution.py:19
  116.7 5.8 collective-permute-done.2
  125.2 7.2 collective-permute-start
  136.4 8.7 %collective-permute-start.2 = (bf16[8,8,8,512]{3,2,1,0:T(8,128)(2,1)S(1)}, bf16[8,8,8,512]{3,2,1,0:T(8,128)(2,1)S(1)}, u32[]{:S(2)}, u32[]{:S(2)}) collective-permute-start(bf16[8,8,8,512]{3,2,1,0:T(8,128)(2,1)S(1)} %get-tuple-element.522), channel_id=1, source_target_pairs={{0,32},{32,64},{64,96},{96,128},{128,160},{160,192},{192,224},{1,3... | collective-permute-start | bytes 1572872 | tf_op jit(solution)/shard_map/while/body/eval_jaxpr/ppermute | solution.py:29
  145.3 5.8 collective-permute-done.2
  153.8 7.4 collective-permute-start
  169.7 5.8 collective-permute-done.2
  178.1 6.8 collective-permute-start
  189.0 8.7 %collective-permute-start.2 = (bf16[8,8,8,512]{3,2,1,0:T(8,128)(2,1)S(1)}, bf16[8,8,8,512]{3,2,1,0:T(8,128)(2,1)S(1)}, u32[]{:S(2)}, u32[]{:S(2)}) collective-permute-start(bf16[8,8,8,512]{3,2,1,0:T(8,128)(2,1)S(1)} %get-tuple-element.522), channel_id=1, source_target_pairs={{0,32},{32,64},{64,96},{96,128},{128,160},{160,192},{192,224},{1,3... | collective-permute-start | bytes 1572872 | tf_op jit(solution)/shard_map/while/body/eval_jaxpr/ppermute | solution.py:29
  197.9 5.8 collective-permute-done.2
  206.4 6.8 collective-permute-start
  221.7 5.8 collective-permute-done.2
  230.1 6.8 collective-permute-start
  241.0 10.7 %collective-permute-start.2 = (bf16[8,8,8,512]{3,2,1,0:T(8,128)(2,1)S(1)}, bf16[8,8,8,512]{3,2,1,0:T(8,128)(2,1)S(1)}, u32[]{:S(2)}, u32[]{:S(2)}) collective-permute-start(bf16[8,8,8,512]{3,2,1,0:T(8,128)(2,1)S(1)} %get-tuple-element.522), channel_id=1, source_target_pairs={{0,32},{32,64},{64,96},{96,128},{128,160},{160,192},{192,224},{1,3... | collective-permute-start | bytes 1572872 | tf_op jit(solution)/shard_map/while/body/eval_jaxpr/ppermute | solution.py:29
  258.8 306.7 %while.28 = (s32[]{:T(128)}, bf16[8,8,8,512]{3,2,1,0:T(8,128)(2,1)}, bf16[2,8,8,8,512]{4,3,2,1,0:T(8,128)(2,1)S(1)}, s32[9]{0:T(128)S(1)}, s32[]{:T(128)}, /*ind...) while((s32[]{:T(128)}, ...), condition=%wide.region_7.8_spmd, body=%wide.region_4.7_spmd.sunk | while | flops 2424045568 | bytes 67764888 | solution.py:138
  262.3 6.7 collective-permute-start.3
  275.7 10.3 %collective-permute-done.5 = bf16[8,8,8,512]{3,2,1,0:T(8,128)(2,1)} collective-permute-done((bf16[8,8,8,512]{3,2,1,0:T(8,128)(2,1)S(1)}, bf16[8,8,8,512]{3,2,1,0:T(8,128)(2,1)}, u32[]{:S(2)}, u32[]{:S(2)}) %collective-permute-start.5) | collective-permute-done | bytes 524320 | tf_op jit(solution)/shard_map/while/body/eval_jaxpr/ppermute | solution.py:29
  289.5 6.8 collective-permute-start.3
  302.9 12.0 %collective-permute-done.5 = bf16[8,8,8,512]{3,2,1,0:T(8,128)(2,1)} collective-permute-done((bf16[8,8,8,512]{3,2,1,0:T(8,128)(2,1)S(1)}, bf16[8,8,8,512]{3,2,1,0:T(8,128)(2,1)}, u32[]{:S(2)}, u32[]{:S(2)}) %collective-permute-start.5) | collective-permute-done | bytes 524320 | tf_op jit(solution)/shard_map/while/body/eval_jaxpr/ppermute | solution.py:29
  318.5 6.8 collective-permute-start.3
  331.9 10.5 %collective-permute-done.5 = bf16[8,8,8,512]{3,2,1,0:T(8,128)(2,1)} collective-permute-done((bf16[8,8,8,512]{3,2,1,0:T(8,128)(2,1)S(1)}, bf16[8,8,8,512]{3,2,1,0:T(8,128)(2,1)}, u32[]{:S(2)}, u32[]{:S(2)}) %collective-permute-start.5) | collective-permute-done | bytes 524320 | tf_op jit(solution)/shard_map/while/body/eval_jaxpr/ppermute | solution.py:29
  345.9 6.8 collective-permute-start.3
  359.3 12.0 %collective-permute-done.5 = bf16[8,8,8,512]{3,2,1,0:T(8,128)(2,1)} collective-permute-done((bf16[8,8,8,512]{3,2,1,0:T(8,128)(2,1)S(1)}, bf16[8,8,8,512]{3,2,1,0:T(8,128)(2,1)}, u32[]{:S(2)}, u32[]{:S(2)}) %collective-permute-start.5) | collective-permute-done | bytes 524320 | tf_op jit(solution)/shard_map/while/body/eval_jaxpr/ppermute | solution.py:29
  374.9 6.8 collective-permute-start.3
  388.3 10.0 %collective-permute-done.5 = bf16[8,8,8,512]{3,2,1,0:T(8,128)(2,1)} collective-permute-done((bf16[8,8,8,512]{3,2,1,0:T(8,128)(2,1)S(1)}, bf16[8,8,8,512]{3,2,1,0:T(8,128)(2,1)}, u32[]{:S(2)}, u32[]{:S(2)}) %collective-permute-start.5) | collective-permute-done | bytes 524320 | tf_op jit(solution)/shard_map/while/body/eval_jaxpr/ppermute | solution.py:29
  401.8 6.8 collective-permute-start.3
  415.2 12.5 %collective-permute-done.5 = bf16[8,8,8,512]{3,2,1,0:T(8,128)(2,1)} collective-permute-done((bf16[8,8,8,512]{3,2,1,0:T(8,128)(2,1)S(1)}, bf16[8,8,8,512]{3,2,1,0:T(8,128)(2,1)}, u32[]{:S(2)}, u32[]{:S(2)}) %collective-permute-start.5) | collective-permute-done | bytes 524320 | tf_op jit(solution)/shard_map/while/body/eval_jaxpr/ppermute | solution.py:29
  431.3 6.8 collective-permute-start.3
  444.6 54.9 %collective-permute-done.5 = bf16[8,8,8,512]{3,2,1,0:T(8,128)(2,1)} collective-permute-done((bf16[8,8,8,512]{3,2,1,0:T(8,128)(2,1)S(1)}, bf16[8,8,8,512]{3,2,1,0:T(8,128)(2,1)}, u32[]{:S(2)}, u32[]{:S(2)}) %collective-permute-start.5) | collective-permute-done | bytes 524320 | tf_op jit(solution)/shard_map/while/body/eval_jaxpr/ppermute | solution.py:29
  503.1 6.8 collective-permute-start.3
  514.9 6.8 conditional.5
  523.3 10.0 %collective-permute-done.5 = bf16[8,8,8,512]{3,2,1,0:T(8,128)(2,1)} collective-permute-done((bf16[8,8,8,512]{3,2,1,0:T(8,128)(2,1)S(1)}, bf16[8,8,8,512]{3,2,1,0:T(8,128)(2,1)}, u32[]{:S(2)}, u32[]{:S(2)}) %collective-permute-start.5) | collective-permute-done | bytes 524320 | tf_op jit(solution)/shard_map/while/body/eval_jaxpr/ppermute | solution.py:29
  536.8 6.8 collective-permute-start.3
  548.6 6.8 conditional.5
  557.0 8.5 %collective-permute-done.5 = bf16[8,8,8,512]{3,2,1,0:T(8,128)(2,1)} collective-permute-done((bf16[8,8,8,512]{3,2,1,0:T(8,128)(2,1)S(1)}, bf16[8,8,8,512]{3,2,1,0:T(8,128)(2,1)}, u32[]{:S(2)}, u32[]{:S(2)}) %collective-permute-start.5) | collective-permute-done | bytes 524320 | tf_op jit(solution)/shard_map/while/body/eval_jaxpr/ppermute | solution.py:29
  567.7 67.9 %all-reduce.4.cloned.1.call-done = bf16[16,8,8,512]{3,2,0,1:T(8,128)(2,1)} async-done(((bf16[16,8,8,512]{3,2,0,1:T(8,128)(2,1)}), bf16[16,8,8,512]{3,2,0,1:T(8,128)(2,1)}) %all-reduce.4.cloned.1.call-update) | async-done | bytes 1048592 | tf_op jit(solution)/shard_map/psum | solution.py:34
  637.3 79.2 %psum.29 = f32[16,16]{1,0:T(8,128)S(1)} all-reduce(f32[16,16]{1,0:T(8,128)S(1)} %convolution_multiply_fusion.1), channel_id=1, replica_groups=mesh['section'=8,'lon'=32] {'section','lon'}, use_global_device_ids=true, to_apply=%region_9.10 | all-reduce | flops 256 | bytes 2048 | tf_op jit(solution)/shard_map/psum | solution.py:159
  718.1 11.6 %psum.30 = f32[16,16]{1,0:T(8,128)S(1)} all-reduce(f32[16,16]{1,0:T(8,128)S(1)} %convolution_multiply_fusion), channel_id=1, replica_groups=mesh['section'=8,'lon'=32] {'section'}, use_global_device_ids=true, to_apply=%region_10.11 | all-reduce | flops 256 | bytes 2048 | tf_op jit(solution)/shard_map/psum | solution.py:162
  729.7 68.0 %psum.31 = f32[16,16]{1,0:T(8,128)} all-reduce(f32[16,16]{1,0:T(8,128)S(1)} %psum.30), channel_id=1, replica_groups=mesh['section'=8,'lon'=32] {'lon'}, use_global_device_ids=true, to_apply=%region_11.12 | all-reduce | flops 256 | bytes 2048 | tf_op jit(solution)/shard_map/psum | solution.py:162
  (287 shorter events, 203.1 us)
Async XLA Ops:
  7.2 628.4 %all-reduce.4.cloned.1.call-start = ((), (), s32[]{:S(2)}) async-start(), calls=%async_computation | async-start | bytes 2097152 | tf_op jit(solution)/shard_map/psum | solution.py:34
  10.9 6.7 collective-permute-start
  14.2 4.0 collective-permute-start.1
  25.4 7.4 collective-permute-start.2
  35.4 11.0 %collective-permute-start = (bf16[8,8,4,512]{3,2,1,0:T(4,128)(2,1)S(1)}, bf16[8,8,4,512]{3,2,1,0:T(4,128)(2,1)S(1)}, u32[]{:S(2)}, u32[]{:S(2)}) collective-permute-start(bf16[8,8,4,512]{3,2,1,0:T(4,128)(2,1)S(1)} %get-tuple-element.424), channel_id=1, source_target_pairs={{1,0},{2,1},{3,2},{4,3},{5,4},{6,5},{7,6},{8,7},{9,8},{10,9},{11,1... | collective-permute-start | bytes 786440 | tf_op jit(solution)/shard_map/while/body/eval_jaxpr/ppermute | solution.py:19
  44.1 3.9 collective-permute-start.1
  55.2 9.9 %collective-permute-start.2 = (bf16[8,8,8,512]{3,2,1,0:T(8,128)(2,1)S(1)}, bf16[8,8,8,512]{3,2,1,0:T(8,128)(2,1)S(1)}, u32[]{:S(2)}, u32[]{:S(2)}) collective-permute-start(bf16[8,8,8,512]{3,2,1,0:T(8,128)(2,1)S(1)} %get-tuple-element.522), channel_id=1, source_target_pairs={{0,32},{32,64},{64,96},{96,128},{128,160},{160,192},{192,224},{1,3... | collective-permute-start | bytes 1572872 | tf_op jit(solution)/shard_map/while/body/eval_jaxpr/ppermute | solution.py:29
  67.8 10.2 %collective-permute-start = (bf16[8,8,4,512]{3,2,1,0:T(4,128)(2,1)S(1)}, bf16[8,8,4,512]{3,2,1,0:T(4,128)(2,1)S(1)}, u32[]{:S(2)}, u32[]{:S(2)}) collective-permute-start(bf16[8,8,4,512]{3,2,1,0:T(4,128)(2,1)S(1)} %get-tuple-element.424), channel_id=1, source_target_pairs={{1,0},{2,1},{3,2},{4,3},{5,4},{6,5},{7,6},{8,7},{9,8},{10,9},{11,1... | collective-permute-start | bytes 786440 | tf_op jit(solution)/shard_map/while/body/eval_jaxpr/ppermute | solution.py:19
  76.8 3.3 collective-permute-start.1
  80.9 16.7 %collective-permute-start.2 = (bf16[8,8,8,512]{3,2,1,0:T(8,128)(2,1)S(1)}, bf16[8,8,8,512]{3,2,1,0:T(8,128)(2,1)S(1)}, u32[]{:S(2)}, u32[]{:S(2)}) collective-permute-start(bf16[8,8,8,512]{3,2,1,0:T(8,128)(2,1)S(1)} %get-tuple-element.522), channel_id=1, source_target_pairs={{0,32},{32,64},{64,96},{96,128},{128,160},{160,192},{192,224},{1,3... | collective-permute-start | bytes 1572872 | tf_op jit(solution)/shard_map/while/body/eval_jaxpr/ppermute | solution.py:29
  100.2 9.3 %collective-permute-start = (bf16[8,8,4,512]{3,2,1,0:T(4,128)(2,1)S(1)}, bf16[8,8,4,512]{3,2,1,0:T(4,128)(2,1)S(1)}, u32[]{:S(2)}, u32[]{:S(2)}) collective-permute-start(bf16[8,8,4,512]{3,2,1,0:T(4,128)(2,1)S(1)} %get-tuple-element.424), channel_id=1, source_target_pairs={{1,0},{2,1},{3,2},{4,3},{5,4},{6,5},{7,6},{8,7},{9,8},{10,9},{11,1... | collective-permute-start | bytes 786440 | tf_op jit(solution)/shard_map/while/body/eval_jaxpr/ppermute | solution.py:19
  108.3 3.3 collective-permute-start.1
  112.3 10.2 %collective-permute-start.2 = (bf16[8,8,8,512]{3,2,1,0:T(8,128)(2,1)S(1)}, bf16[8,8,8,512]{3,2,1,0:T(8,128)(2,1)S(1)}, u32[]{:S(2)}, u32[]{:S(2)}) collective-permute-start(bf16[8,8,8,512]{3,2,1,0:T(8,128)(2,1)S(1)} %get-tuple-element.522), channel_id=1, source_target_pairs={{0,32},{32,64},{64,96},{96,128},{128,160},{160,192},{192,224},{1,3... | collective-permute-start | bytes 1572872 | tf_op jit(solution)/shard_map/while/body/eval_jaxpr/ppermute | solution.py:29
  125.2 8.3 %collective-permute-start = (bf16[8,8,4,512]{3,2,1,0:T(4,128)(2,1)S(1)}, bf16[8,8,4,512]{3,2,1,0:T(4,128)(2,1)S(1)}, u32[]{:S(2)}, u32[]{:S(2)}) collective-permute-start(bf16[8,8,4,512]{3,2,1,0:T(4,128)(2,1)S(1)} %get-tuple-element.424), channel_id=1, source_target_pairs={{1,0},{2,1},{3,2},{4,3},{5,4},{6,5},{7,6},{8,7},{9,8},{10,9},{11,1... | collective-permute-start | bytes 786440 | tf_op jit(solution)/shard_map/while/body/eval_jaxpr/ppermute | solution.py:19
  132.3 3.3 collective-permute-start.1
  136.4 14.8 %collective-permute-start.2 = (bf16[8,8,8,512]{3,2,1,0:T(8,128)(2,1)S(1)}, bf16[8,8,8,512]{3,2,1,0:T(8,128)(2,1)S(1)}, u32[]{:S(2)}, u32[]{:S(2)}) collective-permute-start(bf16[8,8,8,512]{3,2,1,0:T(8,128)(2,1)S(1)} %get-tuple-element.522), channel_id=1, source_target_pairs={{0,32},{32,64},{64,96},{96,128},{128,160},{160,192},{192,224},{1,3... | collective-permute-start | bytes 1572872 | tf_op jit(solution)/shard_map/while/body/eval_jaxpr/ppermute | solution.py:29
  153.8 8.6 %collective-permute-start = (bf16[8,8,4,512]{3,2,1,0:T(4,128)(2,1)S(1)}, bf16[8,8,4,512]{3,2,1,0:T(4,128)(2,1)S(1)}, u32[]{:S(2)}, u32[]{:S(2)}) collective-permute-start(bf16[8,8,4,512]{3,2,1,0:T(4,128)(2,1)S(1)} %get-tuple-element.424), channel_id=1, source_target_pairs={{1,0},{2,1},{3,2},{4,3},{5,4},{6,5},{7,6},{8,7},{9,8},{10,9},{11,1... | collective-permute-start | bytes 786440 | tf_op jit(solution)/shard_map/while/body/eval_jaxpr/ppermute | solution.py:19
  161.2 3.3 collective-permute-start.1
  165.3 10.2 %collective-permute-start.2 = (bf16[8,8,8,512]{3,2,1,0:T(8,128)(2,1)S(1)}, bf16[8,8,8,512]{3,2,1,0:T(8,128)(2,1)S(1)}, u32[]{:S(2)}, u32[]{:S(2)}) collective-permute-start(bf16[8,8,8,512]{3,2,1,0:T(8,128)(2,1)S(1)} %get-tuple-element.522), channel_id=1, source_target_pairs={{0,32},{32,64},{64,96},{96,128},{128,160},{160,192},{192,224},{1,3... | collective-permute-start | bytes 1572872 | tf_op jit(solution)/shard_map/while/body/eval_jaxpr/ppermute | solution.py:29
  178.1 8.0 collective-permute-start
  184.9 3.3 collective-permute-start.1
  189.0 14.8 %collective-permute-start.2 = (bf16[8,8,8,512]{3,2,1,0:T(8,128)(2,1)S(1)}, bf16[8,8,8,512]{3,2,1,0:T(8,128)(2,1)S(1)}, u32[]{:S(2)}, u32[]{:S(2)}) collective-permute-start(bf16[8,8,8,512]{3,2,1,0:T(8,128)(2,1)S(1)} %get-tuple-element.522), channel_id=1, source_target_pairs={{0,32},{32,64},{64,96},{96,128},{128,160},{160,192},{192,224},{1,3... | collective-permute-start | bytes 1572872 | tf_op jit(solution)/shard_map/while/body/eval_jaxpr/ppermute | solution.py:29
  206.4 8.0 collective-permute-start
  213.2 3.3 collective-permute-start.1
  217.3 10.2 %collective-permute-start.2 = (bf16[8,8,8,512]{3,2,1,0:T(8,128)(2,1)S(1)}, bf16[8,8,8,512]{3,2,1,0:T(8,128)(2,1)S(1)}, u32[]{:S(2)}, u32[]{:S(2)}) collective-permute-start(bf16[8,8,8,512]{3,2,1,0:T(8,128)(2,1)S(1)} %get-tuple-element.522), channel_id=1, source_target_pairs={{0,32},{32,64},{64,96},{96,128},{128,160},{160,192},{192,224},{1,3... | collective-permute-start | bytes 1572872 | tf_op jit(solution)/shard_map/while/body/eval_jaxpr/ppermute | solution.py:29
  230.1 8.0 collective-permute-start
  236.9 3.3 collective-permute-start.1
  241.0 16.8 %collective-permute-start.2 = (bf16[8,8,8,512]{3,2,1,0:T(8,128)(2,1)S(1)}, bf16[8,8,8,512]{3,2,1,0:T(8,128)(2,1)S(1)}, u32[]{:S(2)}, u32[]{:S(2)}) collective-permute-start(bf16[8,8,8,512]{3,2,1,0:T(8,128)(2,1)S(1)} %get-tuple-element.522), channel_id=1, source_target_pairs={{0,32},{32,64},{64,96},{96,128},{128,160},{160,192},{192,224},{1,3... | collective-permute-start | bytes 1572872 | tf_op jit(solution)/shard_map/while/body/eval_jaxpr/ppermute | solution.py:29
  262.3 8.2 %collective-permute-start.3 = (bf16[8,8,4,512]{3,2,1,0:T(4,128)(2,1)}, bf16[8,8,4,512]{3,2,1,0:T(4,128)(2,1)}, u32[]{:S(2)}, u32[]{:S(2)}) collective-permute-start(bf16[8,8,4,512]{3,2,1,0:T(4,128)(2,1)} %get-tuple-element.439), channel_id=1, source_target_pairs={{1,0},{2,1},{3,2},{4,3},{5,4},{6,5},{7,6},{8,7},{9,8},{10,9},{11,1... | collective-permute-start | bytes 786440 | tf_op jit(solution)/shard_map/while/body/eval_jaxpr/ppermute | solution.py:19
  269.1 3.3 collective-permute-start.4
  274.2 11.8 %collective-permute-start.5 = (bf16[8,8,8,512]{3,2,1,0:T(8,128)(2,1)S(1)}, bf16[8,8,8,512]{3,2,1,0:T(8,128)(2,1)}, u32[]{:S(2)}, u32[]{:S(2)}) collective-permute-start(bf16[8,8,8,512]{3,2,1,0:T(8,128)(2,1)S(1)} %get-tuple-element.523), channel_id=1, source_target_pairs={{32,0},{64,32},{96,64},{128,96},{160,128},{192,160},{224,192},{33,... | collective-permute-start | bytes 1572872 | tf_op jit(solution)/shard_map/while/body/eval_jaxpr/ppermute | solution.py:29
  289.5 8.3 %collective-permute-start.3 = (bf16[8,8,4,512]{3,2,1,0:T(4,128)(2,1)}, bf16[8,8,4,512]{3,2,1,0:T(4,128)(2,1)}, u32[]{:S(2)}, u32[]{:S(2)}) collective-permute-start(bf16[8,8,4,512]{3,2,1,0:T(4,128)(2,1)} %get-tuple-element.439), channel_id=1, source_target_pairs={{1,0},{2,1},{3,2},{4,3},{5,4},{6,5},{7,6},{8,7},{9,8},{10,9},{11,1... | collective-permute-start | bytes 786440 | tf_op jit(solution)/shard_map/while/body/eval_jaxpr/ppermute | solution.py:19
  296.3 3.3 collective-permute-start.4
  301.4 13.6 %collective-permute-start.5 = (bf16[8,8,8,512]{3,2,1,0:T(8,128)(2,1)S(1)}, bf16[8,8,8,512]{3,2,1,0:T(8,128)(2,1)}, u32[]{:S(2)}, u32[]{:S(2)}) collective-permute-start(bf16[8,8,8,512]{3,2,1,0:T(8,128)(2,1)S(1)} %get-tuple-element.523), channel_id=1, source_target_pairs={{32,0},{64,32},{96,64},{128,96},{160,128},{192,160},{224,192},{33,... | collective-permute-start | bytes 1572872 | tf_op jit(solution)/shard_map/while/body/eval_jaxpr/ppermute | solution.py:29
  318.5 8.3 %collective-permute-start.3 = (bf16[8,8,4,512]{3,2,1,0:T(4,128)(2,1)}, bf16[8,8,4,512]{3,2,1,0:T(4,128)(2,1)}, u32[]{:S(2)}, u32[]{:S(2)}) collective-permute-start(bf16[8,8,4,512]{3,2,1,0:T(4,128)(2,1)} %get-tuple-element.439), channel_id=1, source_target_pairs={{1,0},{2,1},{3,2},{4,3},{5,4},{6,5},{7,6},{8,7},{9,8},{10,9},{11,1... | collective-permute-start | bytes 786440 | tf_op jit(solution)/shard_map/while/body/eval_jaxpr/ppermute | solution.py:19
  330.3 12.0 %collective-permute-start.5 = (bf16[8,8,8,512]{3,2,1,0:T(8,128)(2,1)S(1)}, bf16[8,8,8,512]{3,2,1,0:T(8,128)(2,1)}, u32[]{:S(2)}, u32[]{:S(2)}) collective-permute-start(bf16[8,8,8,512]{3,2,1,0:T(8,128)(2,1)S(1)} %get-tuple-element.523), channel_id=1, source_target_pairs={{32,0},{64,32},{96,64},{128,96},{160,128},{192,160},{224,192},{33,... | collective-permute-start | bytes 1572872 | tf_op jit(solution)/shard_map/while/body/eval_jaxpr/ppermute | solution.py:29
  345.9 8.3 %collective-permute-start.3 = (bf16[8,8,4,512]{3,2,1,0:T(4,128)(2,1)}, bf16[8,8,4,512]{3,2,1,0:T(4,128)(2,1)}, u32[]{:S(2)}, u32[]{:S(2)}) collective-permute-start(bf16[8,8,4,512]{3,2,1,0:T(4,128)(2,1)} %get-tuple-element.439), channel_id=1, source_target_pairs={{1,0},{2,1},{3,2},{4,3},{5,4},{6,5},{7,6},{8,7},{9,8},{10,9},{11,1... | collective-permute-start | bytes 786440 | tf_op jit(solution)/shard_map/while/body/eval_jaxpr/ppermute | solution.py:19
  357.8 13.6 %collective-permute-start.5 = (bf16[8,8,8,512]{3,2,1,0:T(8,128)(2,1)S(1)}, bf16[8,8,8,512]{3,2,1,0:T(8,128)(2,1)}, u32[]{:S(2)}, u32[]{:S(2)}) collective-permute-start(bf16[8,8,8,512]{3,2,1,0:T(8,128)(2,1)S(1)} %get-tuple-element.523), channel_id=1, source_target_pairs={{32,0},{64,32},{96,64},{128,96},{160,128},{192,160},{224,192},{33,... | collective-permute-start | bytes 1572872 | tf_op jit(solution)/shard_map/while/body/eval_jaxpr/ppermute | solution.py:29
  374.9 8.3 %collective-permute-start.3 = (bf16[8,8,4,512]{3,2,1,0:T(4,128)(2,1)}, bf16[8,8,4,512]{3,2,1,0:T(4,128)(2,1)}, u32[]{:S(2)}, u32[]{:S(2)}) collective-permute-start(bf16[8,8,4,512]{3,2,1,0:T(4,128)(2,1)} %get-tuple-element.439), channel_id=1, source_target_pairs={{1,0},{2,1},{3,2},{4,3},{5,4},{6,5},{7,6},{8,7},{9,8},{10,9},{11,1... | collective-permute-start | bytes 786440 | tf_op jit(solution)/shard_map/while/body/eval_jaxpr/ppermute | solution.py:19
  386.7 11.5 %collective-permute-start.5 = (bf16[8,8,8,512]{3,2,1,0:T(8,128)(2,1)S(1)}, bf16[8,8,8,512]{3,2,1,0:T(8,128)(2,1)}, u32[]{:S(2)}, u32[]{:S(2)}) collective-permute-start(bf16[8,8,8,512]{3,2,1,0:T(8,128)(2,1)S(1)} %get-tuple-element.523), channel_id=1, source_target_pairs={{32,0},{64,32},{96,64},{128,96},{160,128},{192,160},{224,192},{33,... | collective-permute-start | bytes 1572872 | tf_op jit(solution)/shard_map/while/body/eval_jaxpr/ppermute | solution.py:29
  401.8 8.3 %collective-permute-start.3 = (bf16[8,8,4,512]{3,2,1,0:T(4,128)(2,1)}, bf16[8,8,4,512]{3,2,1,0:T(4,128)(2,1)}, u32[]{:S(2)}, u32[]{:S(2)}) collective-permute-start(bf16[8,8,4,512]{3,2,1,0:T(4,128)(2,1)} %get-tuple-element.439), channel_id=1, source_target_pairs={{1,0},{2,1},{3,2},{4,3},{5,4},{6,5},{7,6},{8,7},{9,8},{10,9},{11,1... | collective-permute-start | bytes 786440 | tf_op jit(solution)/shard_map/while/body/eval_jaxpr/ppermute | solution.py:19
  413.7 14.0 %collective-permute-start.5 = (bf16[8,8,8,512]{3,2,1,0:T(8,128)(2,1)S(1)}, bf16[8,8,8,512]{3,2,1,0:T(8,128)(2,1)}, u32[]{:S(2)}, u32[]{:S(2)}) collective-permute-start(bf16[8,8,8,512]{3,2,1,0:T(8,128)(2,1)S(1)} %get-tuple-element.523), channel_id=1, source_target_pairs={{32,0},{64,32},{96,64},{128,96},{160,128},{192,160},{224,192},{33,... | collective-permute-start | bytes 1572872 | tf_op jit(solution)/shard_map/while/body/eval_jaxpr/ppermute | solution.py:29
  431.3 8.3 %collective-permute-start.3 = (bf16[8,8,4,512]{3,2,1,0:T(4,128)(2,1)}, bf16[8,8,4,512]{3,2,1,0:T(4,128)(2,1)}, u32[]{:S(2)}, u32[]{:S(2)}) collective-permute-start(bf16[8,8,4,512]{3,2,1,0:T(4,128)(2,1)} %get-tuple-element.439), channel_id=1, source_target_pairs={{1,0},{2,1},{3,2},{4,3},{5,4},{6,5},{7,6},{8,7},{9,8},{10,9},{11,1... | collective-permute-start | bytes 786440 | tf_op jit(solution)/shard_map/while/body/eval_jaxpr/ppermute | solution.py:19
  443.1 56.5 %collective-permute-start.5 = (bf16[8,8,8,512]{3,2,1,0:T(8,128)(2,1)S(1)}, bf16[8,8,8,512]{3,2,1,0:T(8,128)(2,1)}, u32[]{:S(2)}, u32[]{:S(2)}) collective-permute-start(bf16[8,8,8,512]{3,2,1,0:T(8,128)(2,1)S(1)} %get-tuple-element.523), channel_id=1, source_target_pairs={{32,0},{64,32},{96,64},{128,96},{160,128},{192,160},{224,192},{33,... | collective-permute-start | bytes 1572872 | tf_op jit(solution)/shard_map/while/body/eval_jaxpr/ppermute | solution.py:29
  503.1 8.3 %collective-permute-start.3 = (bf16[8,8,4,512]{3,2,1,0:T(4,128)(2,1)}, bf16[8,8,4,512]{3,2,1,0:T(4,128)(2,1)}, u32[]{:S(2)}, u32[]{:S(2)}) collective-permute-start(bf16[8,8,4,512]{3,2,1,0:T(4,128)(2,1)} %get-tuple-element.439), channel_id=1, source_target_pairs={{1,0},{2,1},{3,2},{4,3},{5,4},{6,5},{7,6},{8,7},{9,8},{10,9},{11,1... | collective-permute-start | bytes 786440 | tf_op jit(solution)/shard_map/while/body/eval_jaxpr/ppermute | solution.py:19
  521.8 11.5 %collective-permute-start.5 = (bf16[8,8,8,512]{3,2,1,0:T(8,128)(2,1)S(1)}, bf16[8,8,8,512]{3,2,1,0:T(8,128)(2,1)}, u32[]{:S(2)}, u32[]{:S(2)}) collective-permute-start(bf16[8,8,8,512]{3,2,1,0:T(8,128)(2,1)S(1)} %get-tuple-element.523), channel_id=1, source_target_pairs={{32,0},{64,32},{96,64},{128,96},{160,128},{192,160},{224,192},{33,... | collective-permute-start | bytes 1572872 | tf_op jit(solution)/shard_map/while/body/eval_jaxpr/ppermute | solution.py:29
  536.8 8.3 %collective-permute-start.3 = (bf16[8,8,4,512]{3,2,1,0:T(4,128)(2,1)}, bf16[8,8,4,512]{3,2,1,0:T(4,128)(2,1)}, u32[]{:S(2)}, u32[]{:S(2)}) collective-permute-start(bf16[8,8,4,512]{3,2,1,0:T(4,128)(2,1)} %get-tuple-element.439), channel_id=1, source_target_pairs={{1,0},{2,1},{3,2},{4,3},{5,4},{6,5},{7,6},{8,7},{9,8},{10,9},{11,1... | collective-permute-start | bytes 786440 | tf_op jit(solution)/shard_map/while/body/eval_jaxpr/ppermute | solution.py:19
  555.5 10.0 %collective-permute-start.5 = (bf16[8,8,8,512]{3,2,1,0:T(8,128)(2,1)S(1)}, bf16[8,8,8,512]{3,2,1,0:T(8,128)(2,1)}, u32[]{:S(2)}, u32[]{:S(2)}) collective-permute-start(bf16[8,8,8,512]{3,2,1,0:T(8,128)(2,1)S(1)} %get-tuple-element.523), channel_id=1, source_target_pairs={{32,0},{64,32},{96,64},{128,96},{160,128},{192,160},{224,192},{33,... | collective-permute-start | bytes 1572872 | tf_op jit(solution)/shard_map/while/body/eval_jaxpr/ppermute | solution.py:29
  (15 other events, 995.1 us)
Sparse Core Ops, SparseCore 0:
  566.8 68.7 all-reduce.3
